TPU v7x, 32 devices: a whole 2x2x4 slice. The times are simulated.
32 devices in a mesh: slab: 32 (over z, y, x, core).
Axes of the slice: x: 2, y: 2, z: 4, core: 2. Of those that a mesh axis runs over, the one named last changes fastest.
Arguments:
- diag_tiles: float32 [128, 256, 256], P('slab'), may hold values from 0 to 1, as said below
- coupling: float32 [128, 256, 256], P('slab'), may hold values from 0 to 1, as said below
- labels: int32 [32768], P('slab'), may hold values from 0 to 511
- confidence: float32 [32768], P('slab'), may hold values from 0.25 to 4
Outputs:
- propagated: float32 [32768, 512], P('slab')
Inputs may be any that keep to these rules, and one draw needn't show every extreme that they name: diag_tiles[i] is symmetric with a zero diagonal and non-negative entries; the symmetric matrix with blocks diag_tiles[i] on the diagonal, coupling[i] below it and its transpose above it (i >= 1) has spectral radius at most 1. `coupling`: all entries are non-negative.
All inputs are finite; a program needn't handle non-finite values.
Results may differ from a plain program's by a relative error of at most 0.0003.
Values sent between devices are 32-bit elements; how exact they have to be, the bound alone decides.
No kernel may reach another device: no remote copies, remote signals or barrier semaphores. Data moves between devices by JAX's collectives and lax.ppermute only.
A program may use at most 128 MiB of HBM per device.

v0:
```python
import functools

import jax
import jax.numpy as jnp
from jax import lax
from jax.experimental import pallas as pl
from jax.experimental.pallas import tpu as pltpu
from jax.sharding import PartitionSpec as P

C = 512

alpha_rate = 0.995

f32 = jnp.float32
bf16 = jnp.bfloat16

NN = (((1,), (0,)), ((), ()))
NT = (((1,), (1,)), ((), ()))
TN = (((0,), (0,)), ((), ()))


def product(left, right, dims=NN):
    return lax.dot_general(left, right, dims, precision=lax.Precision.HIGHEST, preferred_element_type=f32)


def single(left, right, dims=NN):
    return lax.dot_general(left, right, dims, preferred_element_type=f32)


def halves(array):
    high = array.astype(bf16)
    return high, (array - high.astype(f32)).astype(bf16)


def product3(left, right, dims=NN):
    left_high, left_low = halves(left)
    right_high, right_low = halves(right)
    return single(left_high, right_high, dims) + (
        single(left_high, right_low, dims) + single(left_low, right_high, dims)
    )


def narrow_product(left, right):
    return single(left.astype(bf16), right.astype(bf16))


def unit(width):
    rows = lax.broadcasted_iota(jnp.int32, (width, width), 0)
    columns = lax.broadcasted_iota(jnp.int32, (width, width), 1)
    return (rows == columns).astype(f32)


DOUBLINGS = 6


def inverses(matrices):
    width = matrices[0].shape[0]
    identity = unit(width)
    scale = 1.0 / alpha_rate
    residuals = [identity - matrix for matrix in matrices]
    results = [identity for _ in matrices]
    for step in range(DOUBLINGS):
        following = 2.0 * scale * scale - 1.0
        gain = 2.0 * scale * scale / following
        for i, (residual, result) in enumerate(zip(residuals, results)):
            high, low = halves(residual)
            both = jnp.concatenate([high, low], axis=1)

            def times(left_high, left_low):
                wide = single(left_high, both)
                return wide[:, :width] + (wide[:, width:] + single(left_low, high))

            if step < DOUBLINGS - 1:
                residuals[i] = gain * times(high, low) - identity * (1.0 / following)
            results[i] = gain * (result + (times(*halves(result)) if step else residual))
        scale = following
    errors = [identity - product(matrix, result) for matrix, result in zip(matrices, results)]
    squares = [narrow_product(error, error) for error in errors]
    cubes = [narrow_product(error, square) for error, square in zip(errors, squares)]
    return [
        result + product3(result, error + (square + cube))
        for result, error, square, cube in zip(results, errors, squares, cubes)
    ]


def call(kernel, shapes, operands, microseconds, scratch=(), hbm=(), out_hbm=(), alias={}):
    in_specs = [pl.BlockSpec(memory_space=pltpu.VMEM) for _ in operands]
    in_specs[0] = pl.BlockSpec(memory_space=pltpu.SMEM)
    for index in hbm:
        in_specs[index] = pl.BlockSpec(memory_space=pltpu.HBM)
    return pl.pallas_call(
        kernel,
        out_shape=[pltpu.HBM(s, f32) if i in out_hbm else jax.ShapeDtypeStruct(s, f32) for i, s in enumerate(shapes)],
        in_specs=in_specs,
        out_specs=[pl.BlockSpec(memory_space=pltpu.HBM if i in out_hbm else pltpu.VMEM) for i in range(len(shapes))],
        input_output_aliases=alias,
        scratch_shapes=[pltpu.VMEM(shape, f32) if isinstance(shape, tuple) else shape for shape in scratch],
        cost_estimate=pl.CostEstimate(flops=int(microseconds * 1.1e9), bytes_accessed=0, transcendentals=0),
        compiler_params=pltpu.CompilerParams(vmem_limit_bytes=12 * 2**20),
    )(*operands)


def join_rows(target, mine, other, core):
    half = mine.shape[-2]
    target[..., pl.ds(pl.multiple_of(core * half, half), half), :] = mine[...]
    target[..., pl.ds(pl.multiple_of((1 - core) * half, half), half), :] = other[...]


def pack(matrix, out):
    half = matrix.shape[0] // 2
    rows = lax.broadcasted_iota(jnp.int32, (half, half), 0)
    columns = lax.broadcasted_iota(jnp.int32, (half, half), 1)
    last = matrix[half:, half:]
    out[:half, :half] = matrix[half:, :half]
    out[:half, half:] = jnp.where(rows >= columns, matrix[:half, :half], last)
    diagonal = jnp.sum(jnp.where(rows == columns, last, 0.0), axis=0, keepdims=True)
    out[half:, half:] = jnp.broadcast_to(diagonal, (8, half))
    out[half:, :half] = jnp.zeros((8, half), f32)


def unpack(packed):
    half = packed.shape[1] // 2
    rows = lax.broadcasted_iota(jnp.int32, (half, half), 0)
    columns = lax.broadcasted_iota(jnp.int32, (half, half), 1)
    corner = packed[:half, :half]
    both = packed[:half, half:]
    flipped = both.T
    diagonal = packed[half : half + 1, half:]
    first = jnp.where(rows >= columns, both, flipped)
    last = jnp.where(rows < columns, both, jnp.where(rows > columns, flipped, diagonal))
    return jnp.concatenate(
        [jnp.concatenate([first, corner.T], axis=1), jnp.concatenate([corner, last], axis=1)], axis=0
    )


def local_factor(flags, diag_in, coupling_in, inverse_out, link_out, crit, rest, diag, coupling, inner, sems, *, width):
    copies = []
    for i in (0, 2, 1, 3):
        copies.append(pltpu.make_async_copy(diag_in.at[i], diag.at[i], sems.at[i]))
    for i in range(4):
        copies.append(pltpu.make_async_copy(coupling_in.at[i], coupling.at[i], sems.at[4 + i]))
    for copy in copies:
        copy.start()
    identity = unit(width)
    copies[0].wait()
    copies[1].wait()
    v0, v2 = inverses([identity - alpha_rate * diag[0], identity - alpha_rate * diag[2]])
    for copy in copies[2:]:
        copy.wait()
    inner[0] = v0
    inner[2] = v2
    copies = [pltpu.make_async_copy(inner.at[i], inverse_out.at[i], sems.at[8 + i]) for i in range(3)]
    copies[0].start()
    copies[2].start()
    d1 = identity - alpha_rate * diag[1]
    d3 = identity - alpha_rate * diag[3]
    l = [-alpha_rate * coupling[i] for i in range(4)]
    l[0] = jnp.where(flags[1] == 1, 0.0, l[0])
    v0_l1t = product3(v0, l[1], NT)
    v2_l2 = product3(v2, l[2])
    middle = d1 - product3(l[1], v0_l1t) - product3(l[2], v2_l2, TN)
    (v1,) = inverses([middle])
    inner[1] = v1
    copies[1].start()
    v0_l0 = product3(v0, l[0])
    v2_l3t = product3(v2, l[3], NT)
    g = -product3(l[1], v0_l0)
    h = -product3(l[2], v2_l3t, TN)
    v1_g = product3(v1, g)
    v1_h = product3(v1, h)
    left = -product3(l[0], v0_l0, TN) - product3(g, v1_g, TN)
    right = d3 - product3(l[3], v2_l3t) - product3(h, v1_h, TN)
    across = -product3(g, v1_h, TN)
    crit[...] = jnp.where(flags[2] == 0, right, left)
    rest[0] = jnp.where(flags[2] == 0, left, right)
    rest[1] = across
    for i, value in enumerate((v0_l0, v0_l1t, v1_g, v1_h, v2_l2, v2_l3t)):
        link_out[i] = value
    for copy in copies:
        copy.wait()


def local_sides(flags, seeds, link, keep, send, interior, *, width, classes):
    place = lax.broadcasted_iota(jnp.int32, (width, classes), 1).astype(f32)
    turned = seeds[...].T
    b = [jnp.where(turned[:, i : i + 1] == place, turned[:, 4 + i : 5 + i], 0.0) for i in range(4)]

    def from_seeds(index, i):
        chosen = jnp.where(turned[:, i : i + 1] == place, 1.0, 0.0).astype(bf16)
        high, low = halves(link[index] * turned[:, 4 + i : 5 + i])
        return single(high, chosen, TN) + single(low, chosen, TN)

    b1 = b[1] - from_seeds(1, 0) - from_seeds(4, 2)
    left = -from_seeds(0, 0) - product3(link[2], b1, TN)
    right = b[3] - from_seeds(5, 2) - product3(link[3], b1, TN)
    interior[0] = b[0]
    interior[1] = b1
    interior[2] = b[2]
    lower = flags[0] == 0
    half = classes // 2
    crit = jnp.where(lower, right, left)
    rest = jnp.where(lower, left, right)
    keep[0] = jnp.where(lower, crit[:, :half], crit[:, half:])
    keep[1] = jnp.where(lower, rest[:, :half], rest[:, half:])
    send[0] = jnp.where(lower, crit[:, half:], crit[:, :half])
    send[1] = jnp.where(lower, rest[:, half:], rest[:, :half])


def local_spikes(flags, inverse_in, link, sides, spikes, interior, inverse, sem, *, width):
    copy = pltpu.make_async_copy(inverse_in, inverse, sem)
    copy.start()
    s1 = jnp.concatenate([link[2], link[3]], axis=1)
    spikes[1] = s1
    first = -product3(link[1], s1)
    spikes[0, :, :width] = first[:, :width] + link[0]
    spikes[0, :, width:] = first[:, width:]
    last = -product3(link[4], s1)
    spikes[2, :, :width] = last[:, :width]
    spikes[2, :, width:] = last[:, width:] + link[5]
    copy.wait()
    y1 = product3(inverse[1], sides[1])
    interior[1] = y1
    interior[0] = product3(inverse[0], sides[0]) - product3(link[1], y1)
    interior[2] = product3(inverse[2], sides[2]) - product3(link[4], y1)


def level_inverse(flags, crit, received, out, *, packed):
    total = crit[...] + received[...]
    (inverse,) = inverses([unpack(total) if packed else total])
    out[...] = inverse


def gather_packed(packed, mine, other, core):
    rows = mine.shape[0] - 8
    packed[pl.ds(pl.multiple_of(core * rows, 8), rows + 8), :] = mine[...]
    packed[pl.ds(pl.multiple_of((1 - core) * rows, 8), rows + 8), :] = other[...]


def gather_rest(whole, mine, other, core):
    half = whole.shape[1] // 2
    join_rows(whole.at[1], mine.at[:half], other.at[:half], core)
    gather_packed(whole.at[0], mine.at[half:], other.at[half:], core)
    whole[0] = unpack(whole[0, : half + 8, :])


def level_crit(flags, inverse, rest, received, *refs, halved, level):
    if halved:
        other, crit_out, scaled_out, whole = refs
        gather_rest(whole, received, other, flags[0])
        received = whole
    else:
        crit_out, scaled_out = refs
    lower = flags[2 + level] == 0
    next_lower = flags[3 + level] == 0
    from_received = lower == next_lower
    base = jnp.where(from_received, received[0], rest[0])
    link = jnp.where(from_received, received[1], rest[1])
    link = jnp.where(next_lower, link, link.T)
    scaled = product3(inverse[...], link)
    scaled_out[...] = scaled
    pack(base - product3(link, scaled, TN), crit_out)


def level_rest(flags, inverse, scaled, rest, received, back, rest_out, message, packed, *, level):
    lower = flags[2 + level] == 0
    next_lower = flags[3 + level] == 0
    from_received = lower == next_lower
    base = jnp.where(from_received, rest[0], received[0])
    link = jnp.where(from_received, rest[1], received[1])
    near = jnp.where(from_received, received[1], rest[1])
    link = jnp.where(next_lower, link.T, link)
    other = product3(inverse[...], link)
    matrix = base - product3(link, other, TN)
    rest_out[0] = matrix
    to_left = jnp.where(next_lower, other, scaled[...])
    to_right = jnp.where(next_lower, scaled[...], other)
    back[0] = to_left
    back[1] = to_right
    rest_out[1] = -product3(jnp.where(next_lower, link.T, near), to_right)
    half = matrix.shape[0] // 2
    message[:half, :] = rest_out[1, pl.ds(pl.multiple_of(flags[0] * half, half), half), :]
    pack(matrix, packed)
    rows = half // 2
    message[half:, :] = packed[pl.ds(pl.multiple_of(flags[0] * rows, 8), rows + 8), :]


def level_end(flags, inverse, rest, received, other, back, crit_out, end, far, message, whole, *, level):
    gather_rest(whole, received, other, flags[0])
    received = whole
    lower = flags[2 + level] == 0
    a_left = jnp.where(lower, rest[0], received[0])
    b_left = jnp.where(lower, rest[1], received[1])
    c_right = jnp.where(lower, received[0], rest[0])
    b_right = jnp.where(lower, received[1], rest[1])
    to_left = product3(inverse[...], b_left, NT)
    to_right = product3(inverse[...], b_right)
    left = a_left - product3(b_left, to_left)
    right = c_right - product3(b_right, to_right, TN)
    across = -product3(b_left, to_right)
    back[0] = to_left
    back[1] = to_right
    (last,) = inverses([right])
    end[...] = last
    scaled = product3(across, last)
    far[...] = scaled
    pack(jnp.where(flags[3 + level] == 0, right, left - product3(scaled, across, NT)), crit_out)
    rows = message.shape[0] - 8
    message[...] = crit_out[pl.ds(pl.multiple_of(flags[0] * rows, 8), rows + 8), :]


def level_sides(flags, inverse, back, own, received, *refs, level, split, final):
    lower = flags[2 + level] == 0
    g = own[0] + received[0]
    a_left = jnp.where(lower, own[1], received[1])
    c_right = jnp.where(lower, received[1], own[1])
    left = a_left - product3(back[0], g, TN)
    right = c_right - product3(back[1], g, TN)
    next_lower = flags[3 + level] == 0
    if final:
        far, end, value, out, outer = refs
        out[...] = jnp.where(next_lower, right, left - product3(far[...], right))
    else:
        crit = jnp.where(next_lower, right, left)
        rest = jnp.where(next_lower, left, right)
        if split:
            value, keep, send = refs
            half = crit.shape[1] // 2
            for i, side in enumerate((crit, rest)):
                keep[i] = jnp.where(next_lower, side[:, :half], side[:, half:])
                send[i] = jnp.where(next_lower, side[:, half:], side[:, :half])
        else:
            value, out = refs
            out[0] = crit
            out[1] = rest
    value[...] = product3(inverse[...], g)
    if final:
        outer[...] = product3(end[...], right)


def root_inverse(flags, crit, mine, other, out, packed):
    gather_packed(packed, mine, other, flags[0])
    (inverse,) = inverses([unpack(crit[...] + packed[...])])
    out[...] = inverse


def descend(flags, *refs, levels):
    root, own, received, far, outer = refs[:5]
    count = levels - 1
    backs, values = refs[5 : 5 + count], refs[5 + count : 5 + 2 * count]
    send, keep, send_near = refs[-3:]
    lower = flags[2 + levels - 1] == 0
    q = product3(root[...], own[...] + received[...])
    outer = outer[...] - product3(far[...], q, TN)
    p = jnp.where(lower, 0.0, q)
    r = jnp.where(lower, q, outer)
    for level in range(levels - 2, -1, -1):
        if level:
            value = values[level][...]
        else:
            half = keep.shape[2]
            value = values[level][:, pl.ds(pl.multiple_of(flags[3] * half, half), half)]
        q = value - product3(backs[level][0], p) - product3(backs[level][1], r)
        lower = flags[2 + level] == 0
        if level == 1:
            send[0] = jnp.where(lower, q, p)
            send[1] = jnp.where(lower, r, q)
        if level == 0:
            send_near[0] = jnp.where(lower, q, p)
            send_near[1] = jnp.where(lower, r, q)
        p, r = jnp.where(lower, p, q), jnp.where(lower, q, r)
    keep[0] = p
    keep[1] = r


def descend_last(flags, mine, back, value, keep, send):
    half = keep.shape[2]
    place = 1 - flags[3]
    p, r = mine[0], mine[1]
    q = value[:, pl.ds(pl.multiple_of(place * half, half), half)] - product3(back[0], p) - product3(back[1], r)
    lower = flags[2] == 0
    keep[0] = jnp.where(lower, p, q)
    keep[1] = jnp.where(lower, q, r)
    send[0] = jnp.where(lower, q, p)
    send[1] = jnp.where(lower, r, q)


def finish(flags, keep, received, spikes, interior, *refs, width, classes, own):
    out, ends, rows, sems = refs[-4:]
    quarter = classes // 4
    place = flags[3] if own else 1 - flags[3]
    columns = [pl.ds(pl.multiple_of(k * 2 * quarter + place * quarter, quarter), quarter) for k in range(2)]
    lower = flags[0] == 0
    copies = []

    def leave(source, block):
        for k in range(2):
            copies.append(
                pltpu.make_async_copy(
                    source.at[:, pl.ds(k * quarter, quarter)],
                    out.at[pl.ds(block * width, width), columns[k]],
                    sems.at[2 * block + k],
                )
            )
            copies[-1].start()

    for i in range(2):
        ends[i * width : (i + 1) * width, :quarter] = jnp.where(lower, keep[i], received[i])
        ends[i * width : (i + 1) * width, quarter:] = jnp.where(lower, received[i], keep[i])
    leave(ends.at[pl.ds(width, width)], 3)
    for i in range(3):
        side = jnp.concatenate([interior[i, :, columns[0]], interior[i, :, columns[1]]], axis=1)
        rows[i] = side - product3(spikes[i], ends[...])
        leave(rows.at[i], i)
    for copy in copies:
        copy.wait()


def swapped(array, distance):
    length = lax.axis_size("slab")
    return lax.ppermute(array, "slab", [(i, i ^ distance) for i in range(length)])


def shards(diag_tiles, coupling, labels, confidence):
    blocks, width, _ = diag_tiles.shape
    classes = C
    square, pair = (width, width), (2, width, width)
    packed, message = (width // 2 + 8, width), (width // 2 + width // 4 + 8, width)
    wide, narrow = (width, classes // 2), (width, classes // 4)
    levels = lax.axis_size("slab").bit_length() - 1
    position = lax.axis_index("slab")
    flags = jnp.stack([position & 1, (position == 0).astype(jnp.int32)] + [(position >> k) & 1 for k in range(levels)])
    seeds = jnp.concatenate([labels.reshape(blocks, width).astype(f32), confidence.reshape(blocks, width)], axis=0)
    diag_tiles = pltpu.with_memory_space_constraint(diag_tiles, pltpu.HBM)
    coupling = pltpu.with_memory_space_constraint(coupling, pltpu.HBM)
    inverse, link, crit, rest = call(
        functools.partial(local_factor, width=width),
        [(3,) + square, (6,) + square, square, pair],
        [flags, diag_tiles, coupling],
        13,
        [(4,) + square, (4,) + square, (3,) + square, pltpu.SemaphoreType.DMA((11,))],
        (1, 2),
        (0,),
    )
    received_crit = swapped(crit, 1)
    received_rest = [swapped(rest, 1)]
    sides, send, inner = call(
        functools.partial(local_sides, width=width, classes=classes),
        [(2,) + wide, (2,) + wide, (3, width, classes)],
        [flags, seeds, link],
        3,
    )
    received_crit, send = lax.optimization_barrier((received_crit, send))
    received_sides = swapped(send, 1)
    backs, values = [], []
    for level in range(levels - 1):
        final = level == levels - 2
        halved = level > 0
        (middle,) = call(
            functools.partial(level_inverse, packed=halved), [square], [flags, crit, received_crit], 4.5
        )
        if halved:
            arrived, middle = lax.optimization_barrier((received_rest, middle))
            received_rest = [arrived, swapped(arrived, 1)]
            if final:
                send, middle = lax.optimization_barrier((send, middle))
        if final:
            back, crit, end, far, message = call(
                functools.partial(level_end, level=level),
                [pair, packed, square, square, (width // 4 + 8, width)],
                [flags, middle, rest] + received_rest,
                7,
                [pair],
            )
            received_crit = swapped(message, 2 ** (level + 1))
        else:
            crit, scaled, *joined = call(
                functools.partial(level_crit, halved=halved, level=level),
                [packed, square] + [pair] * halved,
                [flags, middle, rest] + received_rest,
                1.2,
            )
            if halved:
                crit, send = lax.optimization_barrier((crit, send))
            received_crit = swapped(crit, 2 ** (level + 1))
            back, rest, rest_half = call(
                functools.partial(level_rest, level=level),
                [pair, pair, message],
                [flags, middle, scaled, rest] + (joined or received_rest),
                1.2,
                [packed],
            )
            received_rest = swapped(rest_half, 2 ** (level + 1))
        if halved:
            received_sides = swapped(send, 2**level)
        split = level == 0
        columns = wide if split else narrow
        value, *others = call(
            functools.partial(level_sides, level=level, split=split, final=final),
            [columns] + ([columns, columns] if final else [(2,) + narrow, (2,) + narrow] if split else [(2,) + columns]),
            [flags, middle, back, sides, received_sides] + ([far, end] if final else []),
            0.05 if final else 1,
        )
        if final:
            own, outer = others
            own, inner = lax.optimization_barrier((own, inner))
            spikes, interior = call(
                functools.partial(local_spikes, width=width),
                [(3, width, 2 * width), (3, width, classes)],
                [flags, inverse, link, inner],
                0.05,
                [(3,) + square, pltpu.SemaphoreType.DMA(())],
                (1,),
            )
            received_crit, spikes, interior = lax.optimization_barrier((received_crit, spikes, interior))
            received_own = swapped(own, 2 ** (level + 1))
        else:
            sides, send = others[0], others[-1]
        backs.append(back)
        values.append(value)
    (root,) = call(root_inverse, [square], [flags, crit, received_crit, swapped(received_crit, 1)], 0.05, [packed])
    send, keep, send_near = call(
        functools.partial(descend, levels=levels),
        [(2,) + narrow, (2,) + narrow, (2,) + narrow],
        [flags, root, own, received_own, far, outer] + backs + values,
        2,
    )
    arrived = swapped(send, 2)
    near = swapped(send_near, 1)
    out = []
    for own in (True, False):
        out = call(
            functools.partial(finish, width=width, classes=classes, own=own),
            [(blocks * width, classes)],
            [flags, keep, near, spikes, interior, *out],
            0.05 if own else 2,
            [(2 * width, classes // 2), (3, width, classes // 2), pltpu.SemaphoreType.DMA((8,))],
            () if own else (5,),
            (0,),
            {} if own else {5: 0},
        )
        if own:
            arrived, *out = lax.optimization_barrier((arrived, *out))
            keep, send = call(
                descend_last, [(2,) + narrow, (2,) + narrow], [flags, arrived, backs[0], values[0]], 0.7
            )
            near = swapped(send, 1)
    (out,) = out
    return out


def solution(mesh):
    in_specs = (P("slab", None, None), P("slab", None, None), P("slab"), P("slab"))
    out_specs = P("slab", None)
    return jax.shard_map(shards, mesh=mesh, in_specs=in_specs, out_specs=out_specs, check_vma=False)
```

profile of v0, /device:TPU:1, one launch (start us, length us, event | category | flops | bytes accessed | tf_op | source)
XLA Modules:
  0.0 95.9 jit_solution(7290462029028400010)
XLA Ops:
  0.1 11.0 %shard_map.46 = (f32[3,256,256]{2,1,0:T(8,128)}, f32[6,256,256]{2,1,0:T(8,128)S(1)}, f32[256,256]{1,0:T(8,128)S(1)}, f32[2,256,256]{2,1,0:T(8,128)S(1)}) custom-call(s32[7]{0:T(128)S(1)} %stack.35.flags, f32[4,256,256]{2,1,0:T(8,128)} %diag_in.1, f32[4,256,256]{2,1,0:T(8,128)} %coupling_in.1), custom_call_target="tpu_custom_call" | custom-call | flops 14300000256 | tf_op jit(solution)/shard_map/pallas_call | solution.py:91
  11.7 2.2 %shard_map.47 = (f32[2,256,256]{2,1,0:T(8,128)S(1)}, f32[2,256,256]{2,1,0:T(8,128)S(1)}, f32[3,256,512]{2,1,0:T(8,128)S(1)}) custom-call(s32[7]{0:T(128)S(1)} %stack.35.flags, f32[8,256]{1,0:T(8,128)S(1)} %pad_maximum_fusion.seeds, f32[6,256,256]{2,1,0:T(8,128)S(1)} %get-tuple-element.73.link), custom_call_target="tpu_custom_call" | custom-call | flops 3300000000 | tf_op jit(solution)/shard_map/pallas_call | solution.py:91
  14.0 3.8 %shard_map.48.inverse = f32[256,256]{1,0:T(8,128)S(1)} custom-call(s32[7]{0:T(128)S(1)} %stack.35.flags, f32[256,256]{1,0:T(8,128)S(1)} %get-tuple-element.72.crit, f32[256,256]{1,0:T(8,128)S(1)} %collective-permute-done.received), custom_call_target="tpu_custom_call" | custom-call | flops 4950000128 | tf_op jit(solution)/shard_map/pallas_call | solution.py:91
  19.2 2.4 %collective-permute-start.3 = (f32[136,256]{1,0:T(8,128)S(1)}, f32[136,256]{1,0:T(8,128)S(1)}, u32[]{:S(2)}, u32[]{:S(2)}) collective-permute-start(f32[136,256]{1,0:T(8,128)S(1)} %get-tuple-element.79.crit), channel_id=1, source_target_pairs={{0,2},{1,3},{2,0},{3,1},{4,6},{5,7},{6,4},{7,5},{8,10},{9,11},{10,... | collective-permute-start | bytes 417800 | tf_op jit(solution)/shard_map/ppermute | solution.py:420
  22.2 1.5 %shard_map.50 = (f32[2,256,256]{2,1,0:T(8,128)S(1)}, f32[2,256,256]{2,1,0:T(8,128)S(1)}, f32[200,256]{1,0:T(8,128)S(1)}) custom-call(s32[7]{0:T(128)S(1)} %stack.35.flags, f32[256,256]{1,0:T(8,128)S(1)} %shard_map.48.inverse, f32[256,256]{1,0:T(8,128)S(1)} %get-tuple-element.77.scaled, f32[2,256,256]{2,1,0:T(8,128)S(1)} %get-tuple-element.76.rest, ...), custom_call_target="tpu_custom_call" | custom-call | flops 1320000000 | tf_op jit(solution)/shard_map/pallas_call | solution.py:91
  23.8 1.4 %collective-permute-done.3.received = f32[136,256]{1,0:T(8,128)S(1)} collective-permute-done((f32[136,256]{1,0:T(8,128)S(1)}, f32[136,256]{1,0:T(8,128)S(1)}, u32[]{:S(2)}, u32[]{:S(2)}) %collective-permute-start.3) | collective-permute-done | bytes 139296 | tf_op jit(solution)/shard_map/ppermute | solution.py:420
  25.2 3.9 %shard_map.51.inverse = f32[256,256]{1,0:T(8,128)S(1)} custom-call(s32[7]{0:T(128)S(1)} %stack.35.flags, f32[136,256]{1,0:T(8,128)S(1)} %get-tuple-element.79.crit, f32[136,256]{1,0:T(8,128)S(1)} %collective-permute-done.3.received), custom_call_target="tpu_custom_call" | custom-call | flops 4950000128 | tf_op jit(solution)/shard_map/pallas_call | solution.py:91
  38.7 3.9 %shard_map.55.inverse = f32[256,256]{1,0:T(8,128)S(1)} custom-call(s32[7]{0:T(128)S(1)} %stack.35.flags, f32[136,256]{1,0:T(8,128)S(1)} %get-tuple-element.91.crit, f32[136,256]{1,0:T(8,128)S(1)} %collective-permute-done.7.received), custom_call_target="tpu_custom_call" | custom-call | flops 4950000128 | tf_op jit(solution)/shard_map/pallas_call | solution.py:91
  45.4 1.4 %shard_map.56 = (f32[136,256]{1,0:T(8,128)S(1)}, f32[256,256]{1,0:T(8,128)S(1)}, f32[2,256,256]{2,1,0:T(8,128)S(1)}) custom-call(s32[7]{0:T(128)S(1)} %stack.35.flags, f32[256,256]{1,0:T(8,128)S(1)} %shard_map.55.inverse, f32[2,256,256]{2,1,0:T(8,128)S(1)} %get-tuple-element.93.rest, f32[200,256]{1,0:T(8,128)S(1)} %collective-permute-done.5.received, ...), custom_call_target="tpu_custom_call" | custom-call | flops 1320000000 | tf_op jit(solution)/shard_map/pallas_call | solution.py:91
  46.7 1.4 %collective-permute-start.12 = (f32[136,256]{1,0:T(8,128)S(1)}, f32[136,256]{1,0:T(8,128)S(1)}, u32[]{:S(2)}, u32[]{:S(2)}) collective-permute-start(f32[136,256]{1,0:T(8,128)S(1)} %get-tuple-element.106.crit), channel_id=1, source_target_pairs={{0,8},{1,9},{2,10},{3,11},{4,12},{5,13},{6,14},{7,15},{8,0},{9,1},... | collective-permute-start | bytes 417800 | tf_op jit(solution)/shard_map/ppermute | solution.py:420
  49.7 1.7 %collective-permute-start.10 = (f32[2,256,128]{2,1,0:T(8,128)S(1)}, f32[2,256,128]{2,1,0:T(8,128)S(1)}, u32[]{:S(2)}, u32[]{:S(2)}) collective-permute-start(f32[2,256,128]{2,1,0:T(8,128)S(1)} %get-tuple-element.103.own), channel_id=1, source_target_pairs={{0,4},{1,5},{2,6},{3,7},{4,0},{5,1},{6,2},{7,3},{8,12},{9,13},{10,... | collective-permute-start | bytes 786440 | tf_op jit(solution)/shard_map/ppermute | solution.py:420
  51.3 3.9 %shard_map.60.inverse = f32[256,256]{1,0:T(8,128)S(1)} custom-call(s32[7]{0:T(128)S(1)} %stack.35.flags, f32[136,256]{1,0:T(8,128)S(1)} %get-tuple-element.106.crit, f32[136,256]{1,0:T(8,128)S(1)} %collective-permute-done.12.received), custom_call_target="tpu_custom_call" | custom-call | flops 4950000128 | tf_op jit(solution)/shard_map/pallas_call | solution.py:91
  55.4 2.1 %collective-permute-start.13 = (f32[200,256]{1,0:T(8,128)S(1)}, f32[200,256]{1,0:T(8,128)S(1)}, u32[]{:S(2)}, u32[]{:S(2)}) collective-permute-start(f32[200,256]{1,0:T(8,128)S(1)} %collective-permute-done.11.received), channel_id=1, source_target_pairs={{0,1},{1,0},{2,3},{3,2},{4,5},{5,4},{6,7},{7,6},{8,9},{9,8},{10,11... | collective-permute-start | bytes 614408 | tf_op jit(solution)/shard_map/ppermute | solution.py:420
  58.6 2.3 %collective-permute-start.15 = (f32[2,256,128]{2,1,0:T(8,128)S(1)}, f32[2,256,128]{2,1,0:T(8,128)S(1)}, u32[]{:S(2)}, u32[]{:S(2)}) collective-permute-start(f32[2,256,128]{2,1,0:T(8,128)S(1)} %get-tuple-element.115.own), channel_id=1, source_target_pairs={{0,8},{1,9},{2,10},{3,11},{4,12},{5,13},{6,14},{7,15},{8,0},{9,1},... | collective-permute-start | bytes 786440 | tf_op jit(solution)/shard_map/ppermute | solution.py:420
  60.9 5.4 %shard_map.61 = (f32[2,256,256]{2,1,0:T(8,128)S(1)}, f32[136,256]{1,0:T(8,128)S(1)}, f32[256,256]{1,0:T(8,128)S(1)}, f32[256,256]{1,0:T(8,128)S(1)}, f32[72,256]{1,0:T(8,128)S(1)}) custom-call(s32[7]{0:T(128)S(1)} %stack.35.flags, f32[256,256]{1,0:T(8,128)S(1)} %shard_map.60.inverse, f32[2,256,256]{2,1,0:T(8,128)S(1)} %get-tuple-element.109.rest, ...), custom_call_target="tpu_custom_call" | custom-call | flops 7699999744 | tf_op jit(solution)/shard_map/pallas_call | solution.py:91
  66.2 2.4 %collective-permute-start.14 = (f32[72,256]{1,0:T(8,128)S(1)}, f32[72,256]{1,0:T(8,128)S(1)}, u32[]{:S(2)}, u32[]{:S(2)}) collective-permute-start(f32[72,256]{1,0:T(8,128)S(1)} %get-tuple-element.112), channel_id=1, source_target_pairs={{0,16},{1,17},{2,18},{3,19},{4,20},{5,21},{6,22},{7,23},{8,24},{9,... | collective-permute-start | bytes 221192 | tf_op jit(solution)/shard_map/ppermute | solution.py:420
  68.6 1.5 %shard_map.62 = (f32[256,128]{1,0:T(8,128)S(1)}, f32[256,128]{1,0:T(8,128)S(1)}, f32[256,128]{1,0:T(8,128)S(1)}) custom-call(s32[7]{0:T(128)S(1)} %stack.35.flags, f32[256,256]{1,0:T(8,128)S(1)} %shard_map.60.inverse, f32[2,256,256]{2,1,0:T(8,128)S(1)} %get-tuple-element.114.back.refs_8_, f32[2,256,128]{2,1,0:T(8,128)S(1)} %get-tuple-element.115.own, ...), custom_call_target="tpu_custom_call" | custom-call | flops 55000000 | tf_op jit(solution)/shard_map/pallas_call | solution.py:91
  70.9 2.5 %shard_map.63 = (f32[3,256,512]{2,1,0:T(8,128)S(1)}, f32[3,256,512]{2,1,0:T(8,128)S(1)}) custom-call(s32[7]{0:T(128)S(1)} %stack.35.flags, f32[3,256,256]{2,1,0:T(8,128)S(1)} %copy-done, f32[6,256,256]{2,1,0:T(8,128)S(1)} %get-tuple-element.73.link, f32[3,256,512]{2,1,0:T(8,128)S(1)} %get-tuple-element.120.sides), custom_call_target="tpu_custom_call" | custom-call | flops 55000000 | tf_op jit(solution)/shard_map/pallas_call | solution.py:91
  73.3 1.5 %collective-permute-start.16 = (f32[72,256]{1,0:T(8,128)S(1)}, f32[72,256]{1,0:T(8,128)S(1)}, u32[]{:S(2)}, u32[]{:S(2)}) collective-permute-start(f32[72,256]{1,0:T(8,128)S(1)} %collective-permute-done.14.mine), channel_id=1, source_target_pairs={{0,1},{1,0},{2,3},{3,2},{4,5},{5,4},{6,7},{7,6},{8,9},{9,8},{10,11... | collective-permute-start | bytes 221192 | tf_op jit(solution)/shard_map/ppermute | solution.py:420
  75.8 3.9 %shard_map.64.refs_0_ = f32[256,256]{1,0:T(8,128)S(1)} custom-call(s32[7]{0:T(128)S(1)} %stack.35.flags, f32[136,256]{1,0:T(8,128)S(1)} %get-tuple-element.111.crit, f32[72,256]{1,0:T(8,128)S(1)} %collective-permute-done.14.mine, f32[72,256]{1,0:T(8,128)S(1)} %collective-permute-done.16.other), custom_call_target="tpu_custom_call" | custom-call | flops 55000000 | tf_op jit(solution)/shard_map/pallas_call | solution.py:91
  79.7 2.5 %shard_map.65 = (f32[2,256,128]{2,1,0:T(8,128)S(1)}, f32[2,256,128]{2,1,0:T(8,128)S(1)}, f32[2,256,128]{2,1,0:T(8,128)S(1)}) custom-call(s32[7]{0:T(128)S(1)} %stack.35.flags, f32[256,256]{1,0:T(8,128)S(1)} %shard_map.64.refs_0_, f32[256,128]{1,0:T(8,128)S(1)} %get-tuple-element.124.refs_1_, f32[256,128]{1,0:T(8,128)S(1)} %collective-permute-done.17.refs_2_, ...), custom_call_target="tpu_custom_call" | custom-call | flops 2200000000 | tf_op jit(solution)/shard_map/pallas_call | solution.py:91
  83.8 2.3 %shard_map.66.refs_0_ = f32[1024,512]{1,0:T(8,128)} custom-call(s32[7]{0:T(128)S(1)} %stack.35.flags, f32[2,256,128]{2,1,0:T(8,128)S(1)} %get-tuple-element.131.keep, f32[2,256,128]{2,1,0:T(8,128)S(1)} %collective-permute-done.19.received, f32[3,256,512]{2,1,0:T(8,128)S(1)} %get-tuple-element.133.spikes, f32[3,256,512]{2,1,0:T(8,128)S(1)} %get-tuple-element.134.interior), custom_call_target="tpu_custom_call" | custom-call | flops 55000000 | tf_op jit(solution)/shard_map/pallas_call | solution.py:91
  86.1 4.3 %collective-permute-done.18.mine = f32[2,256,128]{2,1,0:T(8,128)S(1)} collective-permute-done((f32[2,256,128]{2,1,0:T(8,128)S(1)}, f32[2,256,128]{2,1,0:T(8,128)S(1)}, u32[]{:S(2)}, u32[]{:S(2)}) %collective-permute-start.18) | collective-permute-done | bytes 262176 | tf_op jit(solution)/shard_map/ppermute | solution.py:420
  93.5 2.3 %shard_map.68 = f32[1024,512]{1,0:T(8,128)} custom-call(s32[7]{0:T(128)S(1)} %stack.35.flags, f32[2,256,128]{2,1,0:T(8,128)S(1)} %get-tuple-element.136.keep, f32[2,256,128]{2,1,0:T(8,128)S(1)} %collective-permute-done.20.received, f32[3,256,512]{2,1,0:T(8,128)S(1)} %get-tuple-element.133.spikes, ...), custom_call_target="tpu_custom_call", output_to_operand_aliasing={{}: (5, {})} | custom-call | flops 2200000000 | tf_op jit(solution)/shard_map/pallas_call | solution.py:91
  (52 shorter events, 24.2 us)
Async XLA Ops:
  0.1 11.6 %copy-start.1 = (s32[1024]{0:T(1024)S(1)}, s32[1024]{0:T(1024)}, u32[]{:S(2)}) copy-start(s32[1024]{0:T(1024)} %param.6) | copy-start | bytes 12292
  0.1 11.6 %copy-start.2 = (f32[1024]{0:T(1024)S(1)}, f32[1024]{0:T(1024)}, u32[]{:S(2)}) copy-start(f32[1024]{0:T(1024)} %param.7) | copy-start | bytes 12292
  11.1 2.8 %collective-permute-start = (f32[256,256]{1,0:T(8,128)S(1)}, f32[256,256]{1,0:T(8,128)S(1)}, u32[]{:S(2)}, u32[]{:S(2)}) collective-permute-start(f32[256,256]{1,0:T(8,128)S(1)} %get-tuple-element.72.crit), channel_id=1, source_target_pairs={{0,1},{1,0},{2,3},{3,2},{4,5},{5,4},{6,7},{7,6},{8,9},{9,8},{10,11... | collective-permute-start | bytes 786440 | tf_op jit(solution)/shard_map/ppermute | solution.py:420
  11.2 6.6 %collective-permute-start.1 = (f32[2,256,256]{2,1,0:T(8,128)S(1)}, f32[2,256,256]{2,1,0:T(8,128)S(1)}, u32[]{:S(2)}, u32[]{:S(2)}) collective-permute-start(f32[2,256,256]{2,1,0:T(8,128)S(1)} %get-tuple-element.76.rest), channel_id=1, source_target_pairs={{0,1},{1,0},{2,3},{3,2},{4,5},{5,4},{6,7},{7,6},{8,9},{9,8},{10,11... | collective-permute-start | bytes 1572872 | tf_op jit(solution)/shard_map/ppermute | solution.py:420
  19.2 6.0 %collective-permute-start.3 = (f32[136,256]{1,0:T(8,128)S(1)}, f32[136,256]{1,0:T(8,128)S(1)}, u32[]{:S(2)}, u32[]{:S(2)}) collective-permute-start(f32[136,256]{1,0:T(8,128)S(1)} %get-tuple-element.79.crit), channel_id=1, source_target_pairs={{0,2},{1,3},{2,0},{3,1},{4,6},{5,7},{6,4},{7,5},{8,10},{9,11},{10,... | collective-permute-start | bytes 417800 | tf_op jit(solution)/shard_map/ppermute | solution.py:420
  21.5 9.8 %collective-permute-start.6 = (f32[2,256,256]{2,1,0:T(8,128)S(1)}, f32[2,256,256]{2,1,0:T(8,128)S(1)}, u32[]{:S(2)}, u32[]{:S(2)}) collective-permute-start(f32[2,256,256]{2,1,0:T(8,128)S(1)} %get-tuple-element.89), channel_id=1, source_target_pairs={{0,1},{1,0},{2,3},{3,2},{4,5},{5,4},{6,7},{7,6},{8,9},{9,8},{10,11... | collective-permute-start | bytes 1572872 | tf_op jit(solution)/shard_map/ppermute | solution.py:420
  23.7 6.8 %collective-permute-start.2 = (f32[200,256]{1,0:T(8,128)S(1)}, f32[200,256]{1,0:T(8,128)S(1)}, u32[]{:S(2)}, u32[]{:S(2)}) collective-permute-start(f32[200,256]{1,0:T(8,128)S(1)} %get-tuple-element.78), channel_id=1, source_target_pairs={{0,2},{1,3},{2,0},{3,1},{4,6},{5,7},{6,4},{7,5},{8,10},{9,11},{10,... | collective-permute-start | bytes 614408 | tf_op jit(solution)/shard_map/ppermute | solution.py:420
  30.5 1.9 %collective-permute-start.4 = (f32[200,256]{1,0:T(8,128)S(1)}, f32[200,256]{1,0:T(8,128)S(1)}, u32[]{:S(2)}, u32[]{:S(2)}) collective-permute-start(f32[200,256]{1,0:T(8,128)S(1)} %collective-permute-done.2.received), channel_id=1, source_target_pairs={{0,1},{1,0},{2,3},{3,2},{4,5},{5,4},{6,7},{7,6},{8,9},{9,8},{10,11... | collective-permute-start | bytes 614408 | tf_op jit(solution)/shard_map/ppermute | solution.py:420
  33.7 5.0 %collective-permute-start.7 = (f32[136,256]{1,0:T(8,128)S(1)}, f32[136,256]{1,0:T(8,128)S(1)}, u32[]{:S(2)}, u32[]{:S(2)}) collective-permute-start(f32[136,256]{1,0:T(8,128)S(1)} %get-tuple-element.91.crit), channel_id=1, source_target_pairs={{0,4},{1,5},{2,6},{3,7},{4,0},{5,1},{6,2},{7,3},{8,12},{9,13},{10,... | collective-permute-start | bytes 417800 | tf_op jit(solution)/shard_map/ppermute | solution.py:420
  36.4 6.7 %collective-permute-start.5 = (f32[200,256]{1,0:T(8,128)S(1)}, f32[200,256]{1,0:T(8,128)S(1)}, u32[]{:S(2)}, u32[]{:S(2)}) collective-permute-start(f32[200,256]{1,0:T(8,128)S(1)} %get-tuple-element.85), channel_id=1, source_target_pairs={{0,4},{1,5},{2,6},{3,7},{4,0},{5,1},{6,2},{7,3},{8,12},{9,13},{10,... | collective-permute-start | bytes 614408 | tf_op jit(solution)/shard_map/ppermute | solution.py:420
  36.7 7.6 %collective-permute-start.9 = (f32[2,256,128]{2,1,0:T(8,128)S(1)}, f32[2,256,128]{2,1,0:T(8,128)S(1)}, u32[]{:S(2)}, u32[]{:S(2)}) collective-permute-start(f32[2,256,128]{2,1,0:T(8,128)S(1)} %get-tuple-element.100), channel_id=1, source_target_pairs={{0,2},{1,3},{2,0},{3,1},{4,6},{5,7},{6,4},{7,5},{8,10},{9,11},{10,... | collective-permute-start | bytes 786440 | tf_op jit(solution)/shard_map/ppermute | solution.py:420
  43.1 2.2 %collective-permute-start.8 = (f32[200,256]{1,0:T(8,128)S(1)}, f32[200,256]{1,0:T(8,128)S(1)}, u32[]{:S(2)}, u32[]{:S(2)}) collective-permute-start(f32[200,256]{1,0:T(8,128)S(1)} %collective-permute-done.5.received), channel_id=1, source_target_pairs={{0,1},{1,0},{2,3},{3,2},{4,5},{5,4},{6,7},{7,6},{8,9},{9,8},{10,11... | collective-permute-start | bytes 614408 | tf_op jit(solution)/shard_map/ppermute | solution.py:420
  46.7 4.6 %collective-permute-start.12 = (f32[136,256]{1,0:T(8,128)S(1)}, f32[136,256]{1,0:T(8,128)S(1)}, u32[]{:S(2)}, u32[]{:S(2)}) collective-permute-start(f32[136,256]{1,0:T(8,128)S(1)} %get-tuple-element.106.crit), channel_id=1, source_target_pairs={{0,8},{1,9},{2,10},{3,11},{4,12},{5,13},{6,14},{7,15},{8,0},{9,1},... | collective-permute-start | bytes 417800 | tf_op jit(solution)/shard_map/ppermute | solution.py:420
  49.4 6.0 %collective-permute-start.11 = (f32[200,256]{1,0:T(8,128)S(1)}, f32[200,256]{1,0:T(8,128)S(1)}, u32[]{:S(2)}, u32[]{:S(2)}) collective-permute-start(f32[200,256]{1,0:T(8,128)S(1)} %get-tuple-element.105), channel_id=1, source_target_pairs={{0,8},{1,9},{2,10},{3,11},{4,12},{5,13},{6,14},{7,15},{8,0},{9,1},... | collective-permute-start | bytes 614408 | tf_op jit(solution)/shard_map/ppermute | solution.py:420
  49.7 7.8 %collective-permute-start.10 = (f32[2,256,128]{2,1,0:T(8,128)S(1)}, f32[2,256,128]{2,1,0:T(8,128)S(1)}, u32[]{:S(2)}, u32[]{:S(2)}) collective-permute-start(f32[2,256,128]{2,1,0:T(8,128)S(1)} %get-tuple-element.103.own), channel_id=1, source_target_pairs={{0,4},{1,5},{2,6},{3,7},{4,0},{5,1},{6,2},{7,3},{8,12},{9,13},{10,... | collective-permute-start | bytes 786440 | tf_op jit(solution)/shard_map/ppermute | solution.py:420
  55.4 5.5 %collective-permute-start.13 = (f32[200,256]{1,0:T(8,128)S(1)}, f32[200,256]{1,0:T(8,128)S(1)}, u32[]{:S(2)}, u32[]{:S(2)}) collective-permute-start(f32[200,256]{1,0:T(8,128)S(1)} %collective-permute-done.11.received), channel_id=1, source_target_pairs={{0,1},{1,0},{2,3},{3,2},{4,5},{5,4},{6,7},{7,6},{8,9},{9,8},{10,11... | collective-permute-start | bytes 614408 | tf_op jit(solution)/shard_map/ppermute | solution.py:420
  58.6 10.1 %collective-permute-start.15 = (f32[2,256,128]{2,1,0:T(8,128)S(1)}, f32[2,256,128]{2,1,0:T(8,128)S(1)}, u32[]{:S(2)}, u32[]{:S(2)}) collective-permute-start(f32[2,256,128]{2,1,0:T(8,128)S(1)} %get-tuple-element.115.own), channel_id=1, source_target_pairs={{0,8},{1,9},{2,10},{3,11},{4,12},{5,13},{6,14},{7,15},{8,0},{9,1},... | collective-permute-start | bytes 786440 | tf_op jit(solution)/shard_map/ppermute | solution.py:420
  66.2 4.6 %copy-start = (f32[3,256,256]{2,1,0:T(8,128)S(1)}, f32[3,256,256]{2,1,0:T(8,128)}, u32[]{:S(2)}) copy-start(f32[3,256,256]{2,1,0:T(8,128)} %get-tuple-element.113.inverse_in) | copy-start | bytes 2359300
  66.2 7.1 %collective-permute-start.14 = (f32[72,256]{1,0:T(8,128)S(1)}, f32[72,256]{1,0:T(8,128)S(1)}, u32[]{:S(2)}, u32[]{:S(2)}) collective-permute-start(f32[72,256]{1,0:T(8,128)S(1)} %get-tuple-element.112), channel_id=1, source_target_pairs={{0,16},{1,17},{2,18},{3,19},{4,20},{5,21},{6,22},{7,23},{8,24},{9,... | collective-permute-start | bytes 221192 | tf_op jit(solution)/shard_map/ppermute | solution.py:420
  70.1 9.6 %collective-permute-start.17 = (f32[256,128]{1,0:T(8,128)S(1)}, f32[256,128]{1,0:T(8,128)S(1)}, u32[]{:S(2)}, u32[]{:S(2)}) collective-permute-start(f32[256,128]{1,0:T(8,128)S(1)} %get-tuple-element.124.refs_1_), channel_id=1, source_target_pairs={{0,16},{1,17},{2,18},{3,19},{4,20},{5,21},{6,22},{7,23},{8,24},{9,... | collective-permute-start | bytes 393224 | tf_op jit(solution)/shard_map/ppermute | solution.py:420
  73.3 2.4 %collective-permute-start.16 = (f32[72,256]{1,0:T(8,128)S(1)}, f32[72,256]{1,0:T(8,128)S(1)}, u32[]{:S(2)}, u32[]{:S(2)}) collective-permute-start(f32[72,256]{1,0:T(8,128)S(1)} %collective-permute-done.14.mine), channel_id=1, source_target_pairs={{0,1},{1,0},{2,3},{3,2},{4,5},{5,4},{6,7},{7,6},{8,9},{9,8},{10,11... | collective-permute-start | bytes 221192 | tf_op jit(solution)/shard_map/ppermute | solution.py:420
  82.2 1.6 %collective-permute-start.19 = (f32[2,256,128]{2,1,0:T(8,128)S(1)}, f32[2,256,128]{2,1,0:T(8,128)S(1)}, u32[]{:S(2)}, u32[]{:S(2)}) collective-permute-start(f32[2,256,128]{2,1,0:T(8,128)S(1)} %get-tuple-element.132), channel_id=1, source_target_pairs={{0,1},{1,0},{2,3},{3,2},{4,5},{5,4},{6,7},{7,6},{8,9},{9,8},{10,11... | collective-permute-start | bytes 786440 | tf_op jit(solution)/shard_map/ppermute | solution.py:420
  82.6 7.7 %collective-permute-start.18 = (f32[2,256,128]{2,1,0:T(8,128)S(1)}, f32[2,256,128]{2,1,0:T(8,128)S(1)}, u32[]{:S(2)}, u32[]{:S(2)}) collective-permute-start(f32[2,256,128]{2,1,0:T(8,128)S(1)} %get-tuple-element.130), channel_id=1, source_target_pairs={{0,2},{1,3},{2,0},{3,1},{4,6},{5,7},{6,4},{7,5},{8,10},{9,11},{10,... | collective-permute-start | bytes 786440 | tf_op jit(solution)/shard_map/ppermute | solution.py:420
  91.3 2.2 %collective-permute-start.20 = (f32[2,256,128]{2,1,0:T(8,128)S(1)}, f32[2,256,128]{2,1,0:T(8,128)S(1)}, u32[]{:S(2)}, u32[]{:S(2)}) collective-permute-start(f32[2,256,128]{2,1,0:T(8,128)S(1)} %get-tuple-element.137), channel_id=1, source_target_pairs={{0,1},{1,0},{2,3},{3,2},{4,5},{5,4},{6,7},{7,6},{8,9},{9,8},{10,11... | collective-permute-start | bytes 786440 | tf_op jit(solution)/shard_map/ppermute | solution.py:420
where the time goes:
time: 96.4 us; the launch traced here: 95.9 us
  Pallas kernels  61.4 us (64%)
  starting transfers between devices  22.7 us (24%)
  waiting for transfers between devices  11.3 us (12%)
    pallas_call x23, Pallas kernels, call(): pl.pallas_call(kernel, out_shape=[pltpu.HBM(s, f32) if i in out_hbm else...  61.4 us
    ppermute x21, starting transfers between devices, swapped(): lax.ppermute(array, 'slab', [(i, i ^ distance) for i in range(length)])  22.7 us
    ppermute x21, waiting for transfers between devices, swapped(): lax.ppermute(array, 'slab', [(i, i ^ distance) for i in range(length)])  11.3 us
  transfers between devices with their start and end apart: 21, of which 9 were waited for; matrix products, arithmetic and copies ran while one was open for 0% of the time, Pallas kernels for 42%

commit v1 on v0

--- a/solution.py
+++ b/solution.py
@@ -443,14 +443,6 @@
     )
     received_crit = swapped(crit, 1)
     received_rest = [swapped(rest, 1)]
-    sides, send, inner = call(
-        functools.partial(local_sides, width=width, classes=classes),
-        [(2,) + wide, (2,) + wide, (3, width, classes)],
-        [flags, seeds, link],
-        3,
-    )
-    received_crit, send = lax.optimization_barrier((received_crit, send))
-    received_sides = swapped(send, 1)
     backs, values = [], []
     for level in range(levels - 1):
         final = level == levels - 2
@@ -489,6 +481,15 @@
                 1.2,
                 [packed],
             )
+            if level == 0:
+                rest_half, seeds = lax.optimization_barrier((rest_half, seeds))
+                sides, send, inner = call(
+                    functools.partial(local_sides, width=width, classes=classes),
+                    [(2,) + wide, (2,) + wide, (3, width, classes)],
+                    [flags, seeds, link],
+                    0.05,
+                )
+                received_sides = swapped(send, 1)
             received_rest = swapped(rest_half, 2 ** (level + 1))
         if halved:
             received_sides = swapped(send, 2**level)

time: 96.4 us -> 95.9 us (level)
  waiting for transfers between devices: 11.3 us -> 9.38 us
  starting transfers between devices: 22.7 us -> 24.1 us
    ppermute x21, waiting for transfers between devices: 11.3 us -> 9.38 us  [swapped(): lax.ppermute(array, 'slab', [(i, i ^ distance) for i in range(length)])]
    ppermute x21, starting transfers between devices: 22.7 us -> 24.1 us  [swapped(): lax.ppermute(array, 'slab', [(i, i ^ distance) for i in range(length)])]
  transfers between devices with their start and end apart: 21 -> 21, of which waited for: 9 -> 8; matrix products, arithmetic and copies ran while one was open for 0% -> 0% of each run, Pallas kernels for 42% -> 43%
where the time goes in v1:
time: 95.9 us; the launch traced here: 95.4 us
  Pallas kernels  61.4 us (64%)
  starting transfers between devices  24.1 us (25%)
  waiting for transfers between devices  9.38 us (10%)
    pallas_call x23, Pallas kernels, call(): pl.pallas_call(kernel, out_shape=[pltpu.HBM(s, f32) if i in out_hbm else...  61.4 us
    ppermute x21, starting transfers between devices, swapped(): lax.ppermute(array, 'slab', [(i, i ^ distance) for i in range(length)])  24.1 us
    ppermute x21, waiting for transfers between devices, swapped(): lax.ppermute(array, 'slab', [(i, i ^ distance) for i in range(length)])  9.38 us
  transfers between devices with their start and end apart: 21, of which 8 were waited for; matrix products, arithmetic and copies ran while one was open for 0% of the time, Pallas kernels for 43%

profile of v1, /device:TPU:1, one launch (start us, length us, event | category | flops | bytes accessed | tf_op | source)
XLA Modules:
  0.0 95.4 jit_solution(11177603883589409684)
XLA Ops:
  0.1 11.0 %shard_map.46 = (f32[3,256,256]{2,1,0:T(8,128)}, f32[6,256,256]{2,1,0:T(8,128)S(1)}, f32[256,256]{1,0:T(8,128)S(1)}, f32[2,256,256]{2,1,0:T(8,128)S(1)}) custom-call(s32[7]{0:T(128)S(1)} %stack.35.flags, f32[4,256,256]{2,1,0:T(8,128)} %diag_in.1, f32[4,256,256]{2,1,0:T(8,128)} %coupling_in.1), custom_call_target="tpu_custom_call" | custom-call | flops 14300000256 | tf_op jit(solution)/shard_map/pallas_call | solution.py:91
  12.7 3.8 %shard_map.47.inverse = f32[256,256]{1,0:T(8,128)S(1)} custom-call(s32[7]{0:T(128)S(1)} %stack.35.flags, f32[256,256]{1,0:T(8,128)S(1)} %get-tuple-element.72.crit, f32[256,256]{1,0:T(8,128)S(1)} %collective-permute-done.received), custom_call_target="tpu_custom_call" | custom-call | flops 4950000128 | tf_op jit(solution)/shard_map/pallas_call | solution.py:91
  17.9 2.4 %collective-permute-start.3 = (f32[136,256]{1,0:T(8,128)S(1)}, f32[136,256]{1,0:T(8,128)S(1)}, u32[]{:S(2)}, u32[]{:S(2)}) collective-permute-start(f32[136,256]{1,0:T(8,128)S(1)} %get-tuple-element.77.crit), channel_id=1, source_target_pairs={{0,2},{1,3},{2,0},{3,1},{4,6},{5,7},{6,4},{7,5},{8,10},{9,11},{10,... | collective-permute-start | bytes 417800 | tf_op jit(solution)/shard_map/ppermute | solution.py:420
  21.8 2.4 %shard_map.53 = (f32[2,256,256]{2,1,0:T(8,128)S(1)}, f32[2,256,256]{2,1,0:T(8,128)S(1)}, f32[3,256,512]{2,1,0:T(8,128)S(1)}) custom-call(s32[7]{0:T(128)S(1)} %stack.35.flags, f32[8,256]{1,0:T(8,128)S(1)} %pad_maximum_fusion.seeds, f32[6,256,256]{2,1,0:T(8,128)S(1)} %get-tuple-element.87.link), custom_call_target="tpu_custom_call" | custom-call | flops 55000000 | tf_op jit(solution)/shard_map/pallas_call | solution.py:91
  24.9 3.9 %shard_map.50.inverse = f32[256,256]{1,0:T(8,128)S(1)} custom-call(s32[7]{0:T(128)S(1)} %stack.35.flags, f32[136,256]{1,0:T(8,128)S(1)} %get-tuple-element.77.crit, f32[136,256]{1,0:T(8,128)S(1)} %collective-permute-done.3.received), custom_call_target="tpu_custom_call" | custom-call | flops 4950000128 | tf_op jit(solution)/shard_map/pallas_call | solution.py:91
  32.9 1.7 %collective-permute-start.7 = (f32[136,256]{1,0:T(8,128)S(1)}, f32[136,256]{1,0:T(8,128)S(1)}, u32[]{:S(2)}, u32[]{:S(2)}) collective-permute-start(f32[136,256]{1,0:T(8,128)S(1)} %get-tuple-element.91.crit), channel_id=1, source_target_pairs={{0,4},{1,5},{2,6},{3,7},{4,0},{5,1},{6,2},{7,3},{8,12},{9,13},{10,... | collective-permute-start | bytes 417800 | tf_op jit(solution)/shard_map/ppermute | solution.py:420
  36.0 1.7 %collective-permute-start.9 = (f32[2,256,128]{2,1,0:T(8,128)S(1)}, f32[2,256,128]{2,1,0:T(8,128)S(1)}, u32[]{:S(2)}, u32[]{:S(2)}) collective-permute-start(f32[2,256,128]{2,1,0:T(8,128)S(1)} %get-tuple-element.100), channel_id=1, source_target_pairs={{0,2},{1,3},{2,0},{3,1},{4,6},{5,7},{6,4},{7,5},{8,10},{9,11},{10,... | collective-permute-start | bytes 786440 | tf_op jit(solution)/shard_map/ppermute | solution.py:420
  38.3 3.9 %shard_map.55.inverse = f32[256,256]{1,0:T(8,128)S(1)} custom-call(s32[7]{0:T(128)S(1)} %stack.35.flags, f32[136,256]{1,0:T(8,128)S(1)} %get-tuple-element.91.crit, f32[136,256]{1,0:T(8,128)S(1)} %collective-permute-done.7.received), custom_call_target="tpu_custom_call" | custom-call | flops 4950000128 | tf_op jit(solution)/shard_map/pallas_call | solution.py:91
  44.7 1.4 %shard_map.56 = (f32[136,256]{1,0:T(8,128)S(1)}, f32[256,256]{1,0:T(8,128)S(1)}, f32[2,256,256]{2,1,0:T(8,128)S(1)}) custom-call(s32[7]{0:T(128)S(1)} %stack.35.flags, f32[256,256]{1,0:T(8,128)S(1)} %shard_map.55.inverse, f32[2,256,256]{2,1,0:T(8,128)S(1)} %get-tuple-element.93.rest, f32[200,256]{1,0:T(8,128)S(1)} %collective-permute-done.5.received, ...), custom_call_target="tpu_custom_call" | custom-call | flops 1320000000 | tf_op jit(solution)/shard_map/pallas_call | solution.py:91
  46.1 1.6 %collective-permute-start.12 = (f32[136,256]{1,0:T(8,128)S(1)}, f32[136,256]{1,0:T(8,128)S(1)}, u32[]{:S(2)}, u32[]{:S(2)}) collective-permute-start(f32[136,256]{1,0:T(8,128)S(1)} %get-tuple-element.106.crit), channel_id=1, source_target_pairs={{0,8},{1,9},{2,10},{3,11},{4,12},{5,13},{6,14},{7,15},{8,0},{9,1},... | collective-permute-start | bytes 417800 | tf_op jit(solution)/shard_map/ppermute | solution.py:420
  49.1 1.6 %collective-permute-start.10 = (f32[2,256,128]{2,1,0:T(8,128)S(1)}, f32[2,256,128]{2,1,0:T(8,128)S(1)}, u32[]{:S(2)}, u32[]{:S(2)}) collective-permute-start(f32[2,256,128]{2,1,0:T(8,128)S(1)} %get-tuple-element.103.own), channel_id=1, source_target_pairs={{0,4},{1,5},{2,6},{3,7},{4,0},{5,1},{6,2},{7,3},{8,12},{9,13},{10,... | collective-permute-start | bytes 786440 | tf_op jit(solution)/shard_map/ppermute | solution.py:420
  50.6 3.9 %shard_map.60.inverse = f32[256,256]{1,0:T(8,128)S(1)} custom-call(s32[7]{0:T(128)S(1)} %stack.35.flags, f32[136,256]{1,0:T(8,128)S(1)} %get-tuple-element.106.crit, f32[136,256]{1,0:T(8,128)S(1)} %collective-permute-done.12.received), custom_call_target="tpu_custom_call" | custom-call | flops 4950000128 | tf_op jit(solution)/shard_map/pallas_call | solution.py:91
  54.9 2.3 %collective-permute-start.13 = (f32[200,256]{1,0:T(8,128)S(1)}, f32[200,256]{1,0:T(8,128)S(1)}, u32[]{:S(2)}, u32[]{:S(2)}) collective-permute-start(f32[200,256]{1,0:T(8,128)S(1)} %collective-permute-done.11.received), channel_id=1, source_target_pairs={{0,1},{1,0},{2,3},{3,2},{4,5},{5,4},{6,7},{7,6},{8,9},{9,8},{10,11... | collective-permute-start | bytes 614408 | tf_op jit(solution)/shard_map/ppermute | solution.py:420
  58.2 2.3 %collective-permute-start.15 = (f32[2,256,128]{2,1,0:T(8,128)S(1)}, f32[2,256,128]{2,1,0:T(8,128)S(1)}, u32[]{:S(2)}, u32[]{:S(2)}) collective-permute-start(f32[2,256,128]{2,1,0:T(8,128)S(1)} %get-tuple-element.115.own), channel_id=1, source_target_pairs={{0,8},{1,9},{2,10},{3,11},{4,12},{5,13},{6,14},{7,15},{8,0},{9,1},... | collective-permute-start | bytes 786440 | tf_op jit(solution)/shard_map/ppermute | solution.py:420
  60.5 5.4 %shard_map.61 = (f32[2,256,256]{2,1,0:T(8,128)S(1)}, f32[136,256]{1,0:T(8,128)S(1)}, f32[256,256]{1,0:T(8,128)S(1)}, f32[256,256]{1,0:T(8,128)S(1)}, f32[72,256]{1,0:T(8,128)S(1)}) custom-call(s32[7]{0:T(128)S(1)} %stack.35.flags, f32[256,256]{1,0:T(8,128)S(1)} %shard_map.60.inverse, f32[2,256,256]{2,1,0:T(8,128)S(1)} %get-tuple-element.109.rest, ...), custom_call_target="tpu_custom_call" | custom-call | flops 7699999744 | tf_op jit(solution)/shard_map/pallas_call | solution.py:91
  65.9 2.3 %collective-permute-start.14 = (f32[72,256]{1,0:T(8,128)S(1)}, f32[72,256]{1,0:T(8,128)S(1)}, u32[]{:S(2)}, u32[]{:S(2)}) collective-permute-start(f32[72,256]{1,0:T(8,128)S(1)} %get-tuple-element.112), channel_id=1, source_target_pairs={{0,16},{1,17},{2,18},{3,19},{4,20},{5,21},{6,22},{7,23},{8,24},{9,... | collective-permute-start | bytes 221192 | tf_op jit(solution)/shard_map/ppermute | solution.py:420
  68.2 1.5 %shard_map.62 = (f32[256,128]{1,0:T(8,128)S(1)}, f32[256,128]{1,0:T(8,128)S(1)}, f32[256,128]{1,0:T(8,128)S(1)}) custom-call(s32[7]{0:T(128)S(1)} %stack.35.flags, f32[256,256]{1,0:T(8,128)S(1)} %shard_map.60.inverse, f32[2,256,256]{2,1,0:T(8,128)S(1)} %get-tuple-element.114.back.refs_8_, f32[2,256,128]{2,1,0:T(8,128)S(1)} %get-tuple-element.115.own, ...), custom_call_target="tpu_custom_call" | custom-call | flops 55000000 | tf_op jit(solution)/shard_map/pallas_call | solution.py:91
  70.6 2.5 %shard_map.63 = (f32[3,256,512]{2,1,0:T(8,128)S(1)}, f32[3,256,512]{2,1,0:T(8,128)S(1)}) custom-call(s32[7]{0:T(128)S(1)} %stack.35.flags, f32[3,256,256]{2,1,0:T(8,128)S(1)} %copy-done, f32[6,256,256]{2,1,0:T(8,128)S(1)} %get-tuple-element.87.link, f32[3,256,512]{2,1,0:T(8,128)S(1)} %get-tuple-element.120.sides), custom_call_target="tpu_custom_call" | custom-call | flops 55000000 | tf_op jit(solution)/shard_map/pallas_call | solution.py:91
  75.2 3.9 %shard_map.64.refs_0_ = f32[256,256]{1,0:T(8,128)S(1)} custom-call(s32[7]{0:T(128)S(1)} %stack.35.flags, f32[136,256]{1,0:T(8,128)S(1)} %get-tuple-element.111.crit, f32[72,256]{1,0:T(8,128)S(1)} %collective-permute-done.14.mine, f32[72,256]{1,0:T(8,128)S(1)} %collective-permute-done.16.other), custom_call_target="tpu_custom_call" | custom-call | flops 55000000 | tf_op jit(solution)/shard_map/pallas_call | solution.py:91
  79.2 2.5 %shard_map.65 = (f32[2,256,128]{2,1,0:T(8,128)S(1)}, f32[2,256,128]{2,1,0:T(8,128)S(1)}, f32[2,256,128]{2,1,0:T(8,128)S(1)}) custom-call(s32[7]{0:T(128)S(1)} %stack.35.flags, f32[256,256]{1,0:T(8,128)S(1)} %shard_map.64.refs_0_, f32[256,128]{1,0:T(8,128)S(1)} %get-tuple-element.124.refs_1_, f32[256,128]{1,0:T(8,128)S(1)} %collective-permute-done.17.refs_2_, ...), custom_call_target="tpu_custom_call" | custom-call | flops 2200000000 | tf_op jit(solution)/shard_map/pallas_call | solution.py:91
  82.1 1.5 %collective-permute-start.18 = (f32[2,256,128]{2,1,0:T(8,128)S(1)}, f32[2,256,128]{2,1,0:T(8,128)S(1)}, u32[]{:S(2)}, u32[]{:S(2)}) collective-permute-start(f32[2,256,128]{2,1,0:T(8,128)S(1)} %get-tuple-element.130), channel_id=1, source_target_pairs={{0,2},{1,3},{2,0},{3,1},{4,6},{5,7},{6,4},{7,5},{8,10},{9,11},{10,... | collective-permute-start | bytes 786440 | tf_op jit(solution)/shard_map/ppermute | solution.py:420
  83.6 2.3 %shard_map.66.refs_0_ = f32[1024,512]{1,0:T(8,128)} custom-call(s32[7]{0:T(128)S(1)} %stack.35.flags, f32[2,256,128]{2,1,0:T(8,128)S(1)} %get-tuple-element.131.keep, f32[2,256,128]{2,1,0:T(8,128)S(1)} %collective-permute-done.19.received, f32[3,256,512]{2,1,0:T(8,128)S(1)} %get-tuple-element.133.spikes, f32[3,256,512]{2,1,0:T(8,128)S(1)} %get-tuple-element.134.interior), custom_call_target="tpu_custom_call" | custom-call | flops 55000000 | tf_op jit(solution)/shard_map/pallas_call | solution.py:91
  85.8 4.0 %collective-permute-done.18.mine = f32[2,256,128]{2,1,0:T(8,128)S(1)} collective-permute-done((f32[2,256,128]{2,1,0:T(8,128)S(1)}, f32[2,256,128]{2,1,0:T(8,128)S(1)}, u32[]{:S(2)}, u32[]{:S(2)}) %collective-permute-start.18) | collective-permute-done | bytes 262176 | tf_op jit(solution)/shard_map/ppermute | solution.py:420
  93.0 2.3 %shard_map.68 = f32[1024,512]{1,0:T(8,128)} custom-call(s32[7]{0:T(128)S(1)} %stack.35.flags, f32[2,256,128]{2,1,0:T(8,128)S(1)} %get-tuple-element.136.keep, f32[2,256,128]{2,1,0:T(8,128)S(1)} %collective-permute-done.20.received, f32[3,256,512]{2,1,0:T(8,128)S(1)} %get-tuple-element.133.spikes, ...), custom_call_target="tpu_custom_call", output_to_operand_aliasing={{}: (5, {})} | custom-call | flops 2200000000 | tf_op jit(solution)/shard_map/pallas_call | solution.py:91
  (52 shorter events, 23.1 us)
Async XLA Ops:
  0.1 11.6 %copy-start.1 = (s32[1024]{0:T(1024)S(1)}, s32[1024]{0:T(1024)}, u32[]{:S(2)}) copy-start(s32[1024]{0:T(1024)} %param.6) | copy-start | bytes 12292
  0.1 11.6 %copy-start.2 = (f32[1024]{0:T(1024)S(1)}, f32[1024]{0:T(1024)}, u32[]{:S(2)}) copy-start(f32[1024]{0:T(1024)} %param.7) | copy-start | bytes 12292
  11.1 1.6 %collective-permute-start = (f32[256,256]{1,0:T(8,128)S(1)}, f32[256,256]{1,0:T(8,128)S(1)}, u32[]{:S(2)}, u32[]{:S(2)}) collective-permute-start(f32[256,256]{1,0:T(8,128)S(1)} %get-tuple-element.72.crit), channel_id=1, source_target_pairs={{0,1},{1,0},{2,3},{3,2},{4,5},{5,4},{6,7},{7,6},{8,9},{9,8},{10,11... | collective-permute-start | bytes 786440 | tf_op jit(solution)/shard_map/ppermute | solution.py:420
  11.2 5.3 %collective-permute-start.1 = (f32[2,256,256]{2,1,0:T(8,128)S(1)}, f32[2,256,256]{2,1,0:T(8,128)S(1)}, u32[]{:S(2)}, u32[]{:S(2)}) collective-permute-start(f32[2,256,256]{2,1,0:T(8,128)S(1)} %get-tuple-element.73.rest), channel_id=1, source_target_pairs={{0,1},{1,0},{2,3},{3,2},{4,5},{5,4},{6,7},{7,6},{8,9},{9,8},{10,11... | collective-permute-start | bytes 1572872 | tf_op jit(solution)/shard_map/ppermute | solution.py:420
  17.9 7.0 %collective-permute-start.3 = (f32[136,256]{1,0:T(8,128)S(1)}, f32[136,256]{1,0:T(8,128)S(1)}, u32[]{:S(2)}, u32[]{:S(2)}) collective-permute-start(f32[136,256]{1,0:T(8,128)S(1)} %get-tuple-element.77.crit), channel_id=1, source_target_pairs={{0,2},{1,3},{2,0},{3,1},{4,6},{5,7},{6,4},{7,5},{8,10},{9,11},{10,... | collective-permute-start | bytes 417800 | tf_op jit(solution)/shard_map/ppermute | solution.py:420
  21.7 7.2 %collective-permute-start.2 = (f32[200,256]{1,0:T(8,128)S(1)}, f32[200,256]{1,0:T(8,128)S(1)}, u32[]{:S(2)}, u32[]{:S(2)}) collective-permute-start(f32[200,256]{1,0:T(8,128)S(1)} %get-tuple-element.76), channel_id=1, source_target_pairs={{0,2},{1,3},{2,0},{3,1},{4,6},{5,7},{6,4},{7,5},{8,10},{9,11},{10,... | collective-permute-start | bytes 614408 | tf_op jit(solution)/shard_map/ppermute | solution.py:420
  24.2 7.6 %collective-permute-start.6 = (f32[2,256,256]{2,1,0:T(8,128)S(1)}, f32[2,256,256]{2,1,0:T(8,128)S(1)}, u32[]{:S(2)}, u32[]{:S(2)}) collective-permute-start(f32[2,256,256]{2,1,0:T(8,128)S(1)} %get-tuple-element.89), channel_id=1, source_target_pairs={{0,1},{1,0},{2,3},{3,2},{4,5},{5,4},{6,7},{7,6},{8,9},{9,8},{10,11... | collective-permute-start | bytes 1572872 | tf_op jit(solution)/shard_map/ppermute | solution.py:420
  28.8 1.6 %collective-permute-start.4 = (f32[200,256]{1,0:T(8,128)S(1)}, f32[200,256]{1,0:T(8,128)S(1)}, u32[]{:S(2)}, u32[]{:S(2)}) collective-permute-start(f32[200,256]{1,0:T(8,128)S(1)} %collective-permute-done.2.received), channel_id=1, source_target_pairs={{0,1},{1,0},{2,3},{3,2},{4,5},{5,4},{6,7},{7,6},{8,9},{9,8},{10,11... | collective-permute-start | bytes 614408 | tf_op jit(solution)/shard_map/ppermute | solution.py:420
  32.9 5.4 %collective-permute-start.7 = (f32[136,256]{1,0:T(8,128)S(1)}, f32[136,256]{1,0:T(8,128)S(1)}, u32[]{:S(2)}, u32[]{:S(2)}) collective-permute-start(f32[136,256]{1,0:T(8,128)S(1)} %get-tuple-element.91.crit), channel_id=1, source_target_pairs={{0,4},{1,5},{2,6},{3,7},{4,0},{5,1},{6,2},{7,3},{8,12},{9,13},{10,... | collective-permute-start | bytes 417800 | tf_op jit(solution)/shard_map/ppermute | solution.py:420
  35.9 6.5 %collective-permute-start.5 = (f32[200,256]{1,0:T(8,128)S(1)}, f32[200,256]{1,0:T(8,128)S(1)}, u32[]{:S(2)}, u32[]{:S(2)}) collective-permute-start(f32[200,256]{1,0:T(8,128)S(1)} %get-tuple-element.83), channel_id=1, source_target_pairs={{0,4},{1,5},{2,6},{3,7},{4,0},{5,1},{6,2},{7,3},{8,12},{9,13},{10,... | collective-permute-start | bytes 614408 | tf_op jit(solution)/shard_map/ppermute | solution.py:420
  36.0 7.6 %collective-permute-start.9 = (f32[2,256,128]{2,1,0:T(8,128)S(1)}, f32[2,256,128]{2,1,0:T(8,128)S(1)}, u32[]{:S(2)}, u32[]{:S(2)}) collective-permute-start(f32[2,256,128]{2,1,0:T(8,128)S(1)} %get-tuple-element.100), channel_id=1, source_target_pairs={{0,2},{1,3},{2,0},{3,1},{4,6},{5,7},{6,4},{7,5},{8,10},{9,11},{10,... | collective-permute-start | bytes 786440 | tf_op jit(solution)/shard_map/ppermute | solution.py:420
  42.4 2.3 %collective-permute-start.8 = (f32[200,256]{1,0:T(8,128)S(1)}, f32[200,256]{1,0:T(8,128)S(1)}, u32[]{:S(2)}, u32[]{:S(2)}) collective-permute-start(f32[200,256]{1,0:T(8,128)S(1)} %collective-permute-done.5.received), channel_id=1, source_target_pairs={{0,1},{1,0},{2,3},{3,2},{4,5},{5,4},{6,7},{7,6},{8,9},{9,8},{10,11... | collective-permute-start | bytes 614408 | tf_op jit(solution)/shard_map/ppermute | solution.py:420
  46.1 4.6 %collective-permute-start.12 = (f32[136,256]{1,0:T(8,128)S(1)}, f32[136,256]{1,0:T(8,128)S(1)}, u32[]{:S(2)}, u32[]{:S(2)}) collective-permute-start(f32[136,256]{1,0:T(8,128)S(1)} %get-tuple-element.106.crit), channel_id=1, source_target_pairs={{0,8},{1,9},{2,10},{3,11},{4,12},{5,13},{6,14},{7,15},{8,0},{9,1},... | collective-permute-start | bytes 417800 | tf_op jit(solution)/shard_map/ppermute | solution.py:420
  49.0 5.9 %collective-permute-start.11 = (f32[200,256]{1,0:T(8,128)S(1)}, f32[200,256]{1,0:T(8,128)S(1)}, u32[]{:S(2)}, u32[]{:S(2)}) collective-permute-start(f32[200,256]{1,0:T(8,128)S(1)} %get-tuple-element.105), channel_id=1, source_target_pairs={{0,8},{1,9},{2,10},{3,11},{4,12},{5,13},{6,14},{7,15},{8,0},{9,1},... | collective-permute-start | bytes 614408 | tf_op jit(solution)/shard_map/ppermute | solution.py:420
  49.1 8.1 %collective-permute-start.10 = (f32[2,256,128]{2,1,0:T(8,128)S(1)}, f32[2,256,128]{2,1,0:T(8,128)S(1)}, u32[]{:S(2)}, u32[]{:S(2)}) collective-permute-start(f32[2,256,128]{2,1,0:T(8,128)S(1)} %get-tuple-element.103.own), channel_id=1, source_target_pairs={{0,4},{1,5},{2,6},{3,7},{4,0},{5,1},{6,2},{7,3},{8,12},{9,13},{10,... | collective-permute-start | bytes 786440 | tf_op jit(solution)/shard_map/ppermute | solution.py:420
  54.9 5.6 %collective-permute-start.13 = (f32[200,256]{1,0:T(8,128)S(1)}, f32[200,256]{1,0:T(8,128)S(1)}, u32[]{:S(2)}, u32[]{:S(2)}) collective-permute-start(f32[200,256]{1,0:T(8,128)S(1)} %collective-permute-done.11.received), channel_id=1, source_target_pairs={{0,1},{1,0},{2,3},{3,2},{4,5},{5,4},{6,7},{7,6},{8,9},{9,8},{10,11... | collective-permute-start | bytes 614408 | tf_op jit(solution)/shard_map/ppermute | solution.py:420
  58.2 9.9 %collective-permute-start.15 = (f32[2,256,128]{2,1,0:T(8,128)S(1)}, f32[2,256,128]{2,1,0:T(8,128)S(1)}, u32[]{:S(2)}, u32[]{:S(2)}) collective-permute-start(f32[2,256,128]{2,1,0:T(8,128)S(1)} %get-tuple-element.115.own), channel_id=1, source_target_pairs={{0,8},{1,9},{2,10},{3,11},{4,12},{5,13},{6,14},{7,15},{8,0},{9,1},... | collective-permute-start | bytes 786440 | tf_op jit(solution)/shard_map/ppermute | solution.py:420
  65.9 4.7 %copy-start = (f32[3,256,256]{2,1,0:T(8,128)S(1)}, f32[3,256,256]{2,1,0:T(8,128)}, u32[]{:S(2)}) copy-start(f32[3,256,256]{2,1,0:T(8,128)} %get-tuple-element.113.inverse_in) | copy-start | bytes 2359300
  65.9 7.2 %collective-permute-start.14 = (f32[72,256]{1,0:T(8,128)S(1)}, f32[72,256]{1,0:T(8,128)S(1)}, u32[]{:S(2)}, u32[]{:S(2)}) collective-permute-start(f32[72,256]{1,0:T(8,128)S(1)} %get-tuple-element.112), channel_id=1, source_target_pairs={{0,16},{1,17},{2,18},{3,19},{4,20},{5,21},{6,22},{7,23},{8,24},{9,... | collective-permute-start | bytes 221192 | tf_op jit(solution)/shard_map/ppermute | solution.py:420
  69.6 9.6 %collective-permute-start.17 = (f32[256,128]{1,0:T(8,128)S(1)}, f32[256,128]{1,0:T(8,128)S(1)}, u32[]{:S(2)}, u32[]{:S(2)}) collective-permute-start(f32[256,128]{1,0:T(8,128)S(1)} %get-tuple-element.124.refs_1_), channel_id=1, source_target_pairs={{0,16},{1,17},{2,18},{3,19},{4,20},{5,21},{6,22},{7,23},{8,24},{9,... | collective-permute-start | bytes 393224 | tf_op jit(solution)/shard_map/ppermute | solution.py:420
  73.1 2.2 %collective-permute-start.16 = (f32[72,256]{1,0:T(8,128)S(1)}, f32[72,256]{1,0:T(8,128)S(1)}, u32[]{:S(2)}, u32[]{:S(2)}) collective-permute-start(f32[72,256]{1,0:T(8,128)S(1)} %collective-permute-done.14.mine), channel_id=1, source_target_pairs={{0,1},{1,0},{2,3},{3,2},{4,5},{5,4},{6,7},{7,6},{8,9},{9,8},{10,11... | collective-permute-start | bytes 221192 | tf_op jit(solution)/shard_map/ppermute | solution.py:420
  81.7 1.9 %collective-permute-start.19 = (f32[2,256,128]{2,1,0:T(8,128)S(1)}, f32[2,256,128]{2,1,0:T(8,128)S(1)}, u32[]{:S(2)}, u32[]{:S(2)}) collective-permute-start(f32[2,256,128]{2,1,0:T(8,128)S(1)} %get-tuple-element.132), channel_id=1, source_target_pairs={{0,1},{1,0},{2,3},{3,2},{4,5},{5,4},{6,7},{7,6},{8,9},{9,8},{10,11... | collective-permute-start | bytes 786440 | tf_op jit(solution)/shard_map/ppermute | solution.py:420
  82.1 7.8 %collective-permute-start.18 = (f32[2,256,128]{2,1,0:T(8,128)S(1)}, f32[2,256,128]{2,1,0:T(8,128)S(1)}, u32[]{:S(2)}, u32[]{:S(2)}) collective-permute-start(f32[2,256,128]{2,1,0:T(8,128)S(1)} %get-tuple-element.130), channel_id=1, source_target_pairs={{0,2},{1,3},{2,0},{3,1},{4,6},{5,7},{6,4},{7,5},{8,10},{9,11},{10,... | collective-permute-start | bytes 786440 | tf_op jit(solution)/shard_map/ppermute | solution.py:420
  90.8 2.2 %collective-permute-start.20 = (f32[2,256,128]{2,1,0:T(8,128)S(1)}, f32[2,256,128]{2,1,0:T(8,128)S(1)}, u32[]{:S(2)}, u32[]{:S(2)}) collective-permute-start(f32[2,256,128]{2,1,0:T(8,128)S(1)} %get-tuple-element.137), channel_id=1, source_target_pairs={{0,1},{1,0},{2,3},{3,2},{4,5},{5,4},{6,7},{7,6},{8,9},{9,8},{10,11... | collective-permute-start | bytes 786440 | tf_op jit(solution)/shard_map/ppermute | solution.py:420
